TPU v7x, 32 devices: a whole 2x2x4 slice. The times are simulated.
32 devices in a mesh: space: 4 (over y, x), slot: 8 (over z, core).
Axes of the slice: x: 2, y: 2, z: 4, core: 2. Of those that a mesh axis runs over, the one named last changes fastest.
Arguments:
- control: bfloat16 [1536, 1024], P('slot', 'space'), may hold values from -6 to 6
- block_lists: int32 [32, 2], P('space'), may hold values from 0 to 7, all different within a row; in each aligned block of 8 rows (0 to 7, 8 to 15, ...) at most 2 rows name the same one
- loc_tiles: bfloat16 [32, 2, 128, 128], P('space'), may hold values from -0.375 to 0.375
- ensemble: bfloat16 [8, 1536, 4096], P('slot', None, 'space'), may hold values from -2.5 to 2.5
- obs_col: int32 [8, 8192], P('slot', 'space'), may hold values from 0 to 4095, as said below
- obs_wts: float32 [8, 48, 8192], P('slot', None, 'space'), may hold values from -0.875 to 0.875
- innovation: float32 [8, 8192], P('slot', 'space'), may hold values from -6 to 6
- inv_error: float32 [8, 8192], P('slot', 'space'), may hold values from 1 to 16
Outputs:
- first_grad: float32 [1536, 1024], P('slot', 'space')
- second_grad: float32 [1536, 1024], P('slot', 'space')
Inputs may be any that keep to these rules, and one draw needn't show every extreme that they name: `block_lists`: each grid block lists 2 different control blocks; among the grid blocks of one space index no control block is listed more than twice. `obs_col`: observation j lies in grid columns (j // 2048) * 8 * 128 to that plus 8 * 128 - 1.
All inputs are finite; a program needn't handle non-finite values.
Results may differ from a plain program's by a relative error of at most 0.0003.
Values may be sent and summed in bfloat16 or wider, within the bound.
A program may use at most 64 MiB of HBM per device.

v0:
```python
import jax
import jax.numpy as jnp
from jax import lax
from jax.sharding import PartitionSpec as P

LEV = 48
BLOCK = 128
K = 2
descent_step = 0.5


def per_device(control, block_lists, loc_tiles, ensemble, obs_col, obs_wts, innovation, inv_error):
    member_rows = control.shape[0]
    cell_count = ensemble.shape[2]
    space_count = lax.axis_size("space")
    block_total = control.shape[1] // BLOCK * space_count
    ref_ids = block_lists.reshape(-1)
    tiles_wide = loc_tiles.astype(jnp.float32)
    tiles_flat = tiles_wide.reshape(-1, BLOCK, BLOCK)
    selector = (ref_ids[:, None] == jnp.arange(block_total, dtype=jnp.int32)[None, :]).astype(
        jnp.float32
    )
    local_cols = obs_col[0] - lax.axis_index("space") * cell_count
    pick_table = (jnp.arange(cell_count, dtype=jnp.int32)[:, None] == local_cols[None, :]).astype(
        jnp.float32
    )
    weights = obs_wts[0]
    inverse = inv_error[0]
    observed = innovation[0]
    own_slot = ensemble[0]

    def localize(current):
        gathered = lax.all_gather(current.astype(jnp.float32), "space", axis=1, tiled=True)
        picked = gathered.reshape(member_rows, block_total, BLOCK)[:, ref_ids, :]
        products = jnp.einsum("crj,rij->cri", picked, tiles_flat, precision=lax.Precision.HIGHEST)
        return (
            products.reshape(member_rows, -1, K, BLOCK).sum(axis=2).reshape(member_rows, cell_count)
        )

    def observe(increment):
        seen_values = jnp.dot(increment, pick_table, precision=lax.Precision.HIGHEST)
        modelled = jnp.sum(weights * seen_values, axis=0)
        residual = inverse * (modelled - observed)
        return jnp.dot(weights * residual[None, :], pick_table.T, precision=lax.Precision.HIGHEST)

    def gradient(current):
        updates = localize(current)
        all_updates = lax.all_gather(updates, "slot", axis=0, tiled=True)
        product_full = own_slot.astype(jnp.float32) * all_updates
        increment = jnp.sum(product_full.reshape(-1, LEV, cell_count), axis=0)
        adjoint_obs = observe(increment)
        forcing = lax.psum_scatter(
            own_slot.astype(jnp.float32)
            * jnp.tile(adjoint_obs, (member_rows * lax.axis_size("slot") // LEV, 1)),
            "slot",
            scatter_dimension=0,
            tiled=True,
        )
        grid_cells = forcing.reshape(member_rows, -1, BLOCK)
        products = jnp.einsum(
            "cgi,gkij->cgkj", grid_cells, tiles_wide, precision=lax.Precision.HIGHEST
        )
        control_term = jnp.einsum(
            "rb,crj->cbj",
            selector,
            products.reshape(member_rows, -1, BLOCK),
            precision=lax.Precision.HIGHEST,
        )
        returned = lax.psum_scatter(
            control_term.reshape(member_rows, block_total * BLOCK),
            "space",
            scatter_dimension=1,
            tiled=True,
        )
        return current.astype(jnp.float32) + returned

    first_grad = gradient(control)
    stepped = control.astype(jnp.float32) - descent_step * first_grad
    second_grad = gradient(stepped)
    return (first_grad, second_grad)


def solution(mesh):
    placed = (
        P("slot", "space"),
        P("space", None),
        P("space", None, None, None),
        P("slot", None, "space"),
        P("slot", "space"),
        P("slot", None, "space"),
        P("slot", "space"),
        P("slot", "space"),
    )
    return jax.shard_map(
        per_device,
        mesh=mesh,
        in_specs=placed,
        out_specs=(P("slot", "space"), P("slot", "space")),
        check_vma=False,
    )
```

profile of v0, /device:TPU:0, one launch (start us, length us, event | category | flops | bytes accessed | tf_op | source)
XLA Modules:
  0.0 419.0 jit_solution(14871258517747074934)
XLA Ops:
  7.2 0.0 copy-start
  7.2 0.0 all-gather.3.cloned.1.call-start
  7.2 0.8 copy.38
  8.0 0.1 reshape.94
  8.1 0.9 convert_element_type.7
  9.0 12.7 %all_gather.12 = f32[192,1024]{1,0:T(8,128)S(1)} all-gather(f32[192,256]{1,0:T(8,128)S(1)} %convert_element_type.7), channel_id=1, replica_groups=mesh['space'=4,'slot'=8] {'space'}, dimensions={1}, use_global_device_ids=true | all-gather | bytes 983040 | tf_op jit(solution)/shard_map/all_gather | solution.py:33
  21.7 0.1 copy_bitcast_fusion.5
  21.8 0.7 gather_fusion
  22.4 0.0 copy-done
  22.4 0.0 copy-start.6
  22.4 1.1 bitcast_reduce_fusion.1
  23.6 1.0 copy_bitcast_fusion.3
  24.5 0.0 all-gather.3.cloned.1.call-update
  24.6 0.0 reduce-scatter.5.cloned.1.call-start
  24.6 0.0 copy-done.6
  24.6 65.1 %all-gather.3.cloned.1.call-done = f32[1536,1024]{1,0:T(8,128)} async-done(((f32[192,1024]{1,0:T(8,128)}), f32[1536,1024]{1,0:T(8,128)}) %all-gather.3.cloned.1.call-update) | async-done | bytes 6291472 | tf_op jit(solution)/shard_map/all_gather | solution.py:48
  89.8 8.0 %convert_multiply_fusion.3 = f32[1536,1024]{1,0:T(8,128)} fusion(f32[1536,1024]{1,0:T(8,128)} %all-gather.3.cloned.1.call-done, bf16[1,1536,1024]{2,1,0:T(8,128)(2,1)} %param.11), kind=kLoop, calls=%fused_computation.5 | loop fusion | flops 3145728 | bytes 15728640 | tf_op jit(solution)/shard_map/mul | solution.py:49
  97.8 3.2 reduce_sum.59
  101.0 0.0 copy-start.4
  101.0 0.0 copy-start.5
  101.0 0.0 copy-done.7
  101.1 0.0 copy-start.1
  101.1 3.2 fusion.19
  104.3 0.0 copy-done.4
  104.3 0.0 copy-done.5
  104.3 4.2 %fusion.2 = f32[48,1024]{1,0:T(8,128)S(1)} fusion(s32[2048]{0:T(1024)S(1)} %bitcast.114, f32[1,48,2048]{2,1,0:T(8,128)S(1)} %copy-done.7, f32[2048]{0:T(1024)S(1)} %bitcast.119), kind=kOutput, calls=%fused_computation.9 | convolution fusion | flops 1210155008 | bytes 606208 | tf_op jit(solution)/shard_map/dot_general | solution.py:44
  108.5 3.6 convert_multiply_fusion.2
  112.1 0.0 reduce-scatter.5.cloned.1.call-update
  112.1 0.2 reduce-scatter.7.cloned.1.call-start
  112.3 0.1 eq.34
  112.4 68.3 %reduce-scatter.5.cloned.1.call-done = f32[192,1024]{1,0:T(8,128)} async-done(((f32[1536,1024]{1,0:T(8,128)}), f32[192,1024]{1,0:T(8,128)}) %reduce-scatter.5.cloned.1.call-update) | async-done | bytes 786448 | tf_op jit(solution)/shard_map/reduce_scatter | solution.py:52
  180.7 1.3 copy.58
  182.0 0.8 fusion.26
  182.8 0.0 copy-start.3
  182.8 1.5 fusion.16
  184.3 1.0 copy.77
  185.3 0.0 reduce-scatter.7.cloned.1.call-update
  185.4 0.0 all-gather.5.cloned.1.call-start
  185.4 24.6 %reduce-scatter.7.cloned.1.call-done = f32[192,256]{1,0:T(8,128)} async-done(((f32[192,1024]{1,0:T(8,128)}), f32[192,256]{1,0:T(8,128)}) %reduce-scatter.7.cloned.1.call-update) | async-done | bytes 196624 | tf_op jit(solution)/shard_map/reduce_scatter | solution.py:69
  210.0 1.6 multiply_subtract_fusion
  211.6 11.1 %all_gather.14 = f32[192,1024]{1,0:T(8,128)S(1)} all-gather(f32[192,256]{1,0:T(8,128)S(1)} %get-tuple-element.2), channel_id=1, replica_groups=mesh['space'=4,'slot'=8] {'space'}, dimensions={1}, use_global_device_ids=true | all-gather | bytes 983040 | tf_op jit(solution)/shard_map/all_gather | solution.py:33
  222.7 0.1 copy_bitcast_fusion.4
  222.8 0.7 gather_fusion.1
  223.4 1.1 bitcast_reduce_fusion
  224.6 1.0 copy_bitcast_fusion.2
  225.5 0.0 all-gather.5.cloned.1.call-update
  225.6 0.0 reduce-scatter.9.cloned.1.call-start
  225.6 64.9 %all-gather.5.cloned.1.call-done = f32[1536,1024]{1,0:T(8,128)} async-done(((f32[192,1024]{1,0:T(8,128)}), f32[1536,1024]{1,0:T(8,128)}) %all-gather.5.cloned.1.call-update) | async-done | bytes 6291472 | tf_op jit(solution)/shard_map/all_gather | solution.py:48
  290.5 8.0 %convert_multiply_fusion.1 = f32[1536,1024]{1,0:T(8,128)} fusion(f32[1536,1024]{1,0:T(8,128)} %all-gather.5.cloned.1.call-done, bf16[1,1536,1024]{2,1,0:T(8,128)(2,1)} %param.11), kind=kLoop, calls=%fused_computation.3 | loop fusion | flops 3145728 | bytes 15728640 | tf_op jit(solution)/shard_map/mul | solution.py:49
  298.5 3.2 reduce_sum.63
  301.7 0.0 copy-start.2
  301.7 3.2 fusion.18
  304.9 4.2 %fusion = f32[48,1024]{1,0:T(8,128)S(1)} fusion(s32[2048]{0:T(1024)S(1)} %bitcast.116, f32[1,48,2048]{2,1,0:T(8,128)S(1)} %copy-done.7, f32[2048]{0:T(1024)S(1)} %bitcast.117), kind=kOutput, calls=%fused_computation.7 | convolution fusion | flops 1210155008 | bytes 606208 | tf_op jit(solution)/shard_map/dot_general | solution.py:44
  309.1 3.6 convert_multiply_fusion
  312.7 0.0 reduce-scatter.9.cloned.1.call-update
  312.7 0.0 reduce-scatter.11.cloned.1.call-start
  312.8 68.6 %reduce-scatter.9.cloned.1.call-done = f32[192,1024]{1,0:T(8,128)} async-done(((f32[1536,1024]{1,0:T(8,128)}), f32[192,1024]{1,0:T(8,128)}) %reduce-scatter.9.cloned.1.call-update) | async-done | bytes 786448 | tf_op jit(solution)/shard_map/reduce_scatter | solution.py:52
  381.3 1.3 copy.60
  382.6 0.8 fusion.24
  383.4 1.5 fusion.14
  384.9 1.0 copy.76
  385.9 0.0 reduce-scatter.11.cloned.1.call-update
  385.9 24.6 %reduce-scatter.11.cloned.1.call-done = f32[192,256]{1,0:T(8,128)} async-done(((f32[192,1024]{1,0:T(8,128)}), f32[192,256]{1,0:T(8,128)}) %reduce-scatter.11.cloned.1.call-update) | async-done | bytes 196624 | tf_op jit(solution)/shard_map/reduce_scatter | solution.py:69
  410.6 1.6 add.27
  (9 shorter events, 0.1 us)
Async XLA Ops:
  7.2 15.2 %copy-start = (bf16[8,2,128,128]{3,2,1,0:T(8,128)(2,1)S(1)}, bf16[8,2,128,128]{3,2,1,0:T(8,128)(2,1)}, u32[]{:S(2)}) copy-start(bf16[8,2,128,128]{3,2,1,0:T(8,128)(2,1)} %param.10) | copy-start | bytes 1572868
  7.2 82.6 %all-gather.3.cloned.1.call-start = ((), (), s32[]{:S(2)}) async-start(), calls=%async_computation.4 | async-start | bytes 7077888 | tf_op jit(solution)/shard_map/all_gather | solution.py:48
  22.4 2.2 copy-start.6
  24.6 156.2 %reduce-scatter.5.cloned.1.call-start = ((), (), s32[]{:S(2)}) async-start(), calls=%async_computation.5 | async-start | bytes 7077888 | tf_op jit(solution)/shard_map/reduce_scatter | solution.py:52
  97.8 3.3 copy-start.7
  101.0 3.2 copy-start.4
  101.0 3.2 copy-start.5
  101.1 7.5 %copy-start.1 = (bf16[1,1536,1024]{2,1,0:T(8,128)(2,1)S(1)}, bf16[1,1536,1024]{2,1,0:T(8,128)(2,1)}, u32[]{:S(2)}) copy-start(bf16[1,1536,1024]{2,1,0:T(8,128)(2,1)} %param.11) | copy-start | bytes 9437188
  112.1 97.9 %reduce-scatter.7.cloned.1.call-start = ((), (), s32[]{:S(2)}) async-start(), calls=%async_computation.6 | async-start | bytes 983040 | tf_op jit(solution)/shard_map/reduce_scatter | solution.py:69
  182.8 27.2 %copy-start.3 = (bf16[192,256]{1,0:T(8,128)(2,1)S(1)}, bf16[192,256]{1,0:T(8,128)(2,1)}, u32[]{:S(2)}) copy-start(bf16[192,256]{1,0:T(8,128)(2,1)} %param.8) | copy-start | bytes 294916
  185.4 105.1 %all-gather.5.cloned.1.call-start = ((), (), s32[]{:S(2)}) async-start(), calls=%async_computation.7 | async-start | bytes 7077888 | tf_op jit(solution)/shard_map/all_gather | solution.py:48
  225.6 155.7 %reduce-scatter.9.cloned.1.call-start = ((), (), s32[]{:S(2)}) async-start(), calls=%async_computation.8 | async-start | bytes 7077888 | tf_op jit(solution)/shard_map/reduce_scatter | solution.py:52
  301.7 7.4 %copy-start.2 = (bf16[1,1536,1024]{2,1,0:T(8,128)(2,1)S(1)}, bf16[1,1536,1024]{2,1,0:T(8,128)(2,1)}, u32[]{:S(2)}) copy-start(bf16[1,1536,1024]{2,1,0:T(8,128)(2,1)} %param.11) | copy-start | bytes 9437188
  312.7 97.9 %reduce-scatter.11.cloned.1.call-start = ((), (), s32[]{:S(2)}) async-start(), calls=%async_computation.9 | async-start | bytes 983040 | tf_op jit(solution)/shard_map/reduce_scatter | solution.py:69
Sparse Core Ops, SparseCore 0:
  24.7 65.0 all-gather.2
  112.2 68.4 reduce-scatter.4
  185.5 24.4 reduce-scatter.6
  225.7 64.7 all-gather.4
  312.8 68.4 reduce-scatter.8
  386.1 24.4 reduce-scatter.10
where the time goes:
time: 419 us
  waiting for transfers between devices  316 us (75%)
  other arithmetic  33.8 us (8%)
  blocking collectives  23.7 us (6%)
  matrix products  21.6 us (5%)
  between operations  14.4 us (3%)
  local copies, waits for them, and re-layouts  8.98 us (2%)
    reduce_scatter x2, waiting for transfers between devices, gradient(): lax.psum_scatter(own_slot.astype(jnp.float32) * jnp.tile(adjoint_obs, (me...  137 us
    all_gather x2, waiting for transfers between devices, gradient(): all_updates = lax.all_gather(updates, 'slot', axis=0, tiled=True)  130 us
    reduce_scatter x2, waiting for transfers between devices, gradient(): lax.psum_scatter(control_term.reshape(member_rows, block_total * BLOCK),...  49.2 us
    all_gather x2, blocking collectives, localize(): lax.all_gather(current.astype(jnp.float32), 'space', axis=1, tiled=True)  23.7 us
    mul x2, other arithmetic, gradient(): product_full = own_slot.astype(jnp.float32) * all_updates  16 us
    dot_general x2, matrix products, observe(): jnp.dot(weights * residual[None, :], pick_table.T, precision=lax.Precisio...  8.41 us
  transfers between devices with their start and end apart: 6, of which 6 were waited for; matrix products, arithmetic and copies ran while one was open for 0% of the time, Pallas kernels for 0%

commit v1 on v0

--- a/solution.py
+++ b/solution.py
@@ -30,7 +30,24 @@
     own_slot = ensemble[0]
 
     def localize(current):
-        gathered = lax.all_gather(current.astype(jnp.float32), "space", axis=1, tiled=True)
+        x = current.astype(jnp.float32)
+        count, here, rows = (lax.axis_size("space"), lax.axis_index("space"), x.shape[1])
+        ahead = [(i, (i + 1) % count) for i in range(count)]
+        left = [(i, (i - 1) % count) for i in range(count)]
+        gathered = jnp.zeros((*x.shape[:1], count * rows, *x.shape[1 + 1 :]), x.dtype)
+        gathered = lax.dynamic_update_slice_in_dim(gathered, x, here * rows, axis=1)
+        from_left = from_right = x
+        halfway = count // 2
+        for step in range(1, halfway + 1):
+            from_left = lax.ppermute(from_left, "space", ahead)
+            gathered = lax.dynamic_update_slice_in_dim(
+                gathered, from_left, (here - step) % count * rows, axis=1
+            )
+            if step < count - halfway:
+                from_right = lax.ppermute(from_right, "space", left)
+                gathered = lax.dynamic_update_slice_in_dim(
+                    gathered, from_right, (here + step) % count * rows, axis=1
+                )
         picked = gathered.reshape(member_rows, block_total, BLOCK)[:, ref_ids, :]
         products = jnp.einsum("crj,rij->cri", picked, tiles_flat, precision=lax.Precision.HIGHEST)
         return (

time: 419 us -> 428 us (1.021)
  blocking collectives: 23.7 us -> 0 us
  waiting for transfers between devices: 316 us -> 339 us
  starting transfers between devices: 0.43 us -> 9 us
    all_gather x2 -> x0, blocking collectives: 23.7 us -> none  [localize(): lax.all_gather(current.astype(jnp.float32), 'space', axis=1, tiled=True)]
    ppermute x0 -> x6, waiting for transfers between devices: none -> 22.6 us  [the longest x4 15.3 us: localize(): from_left = lax.ppermute(from_left, 'space', ahead)]
    ppermute x0 -> x6, starting transfers between devices: none -> 8.58 us  [the longest x4 6.07 us: localize(): from_left = lax.ppermute(from_left, 'space', ahead)]
  transfers between devices with their start and end apart: 6 -> 12, of which waited for: 6 -> 12; matrix products, arithmetic and copies ran while one was open for 0% -> 0% of each run, Pallas kernels for 0% -> 0%
where the time goes in v1:
time: 428 us
  waiting for transfers between devices  339 us (79%)
  other arithmetic  34.7 us (8%)
  matrix products  21.6 us (5%)
  between operations  14.5 us (3%)
  local copies, waits for them, and re-layouts  9.18 us (2%)
  starting transfers between devices  9 us (2%)
    reduce_scatter x2, waiting for transfers between devices, gradient(): lax.psum_scatter(own_slot.astype(jnp.float32) * jnp.tile(adjoint_obs, (me...  137 us
    all_gather x2, waiting for transfers between devices, gradient(): all_updates = lax.all_gather(updates, 'slot', axis=0, tiled=True)  130 us
    reduce_scatter x2, waiting for transfers between devices, gradient(): lax.psum_scatter(control_term.reshape(member_rows, block_total * BLOCK),...  49.2 us
    mul x2, other arithmetic, gradient(): product_full = own_slot.astype(jnp.float32) * all_updates  16 us
    ppermute x4, waiting for transfers between devices, localize(): from_left = lax.ppermute(from_left, 'space', ahead)  15.3 us
  transfers between devices with their start and end apart: 12, of which 12 were waited for; matrix products, arithmetic and copies ran while one was open for 0% of the time, Pallas kernels for 0%

profile of v1, /device:TPU:0, one launch (start us, length us, event | category | flops | bytes accessed | tf_op | source)
XLA Modules:
  0.0 428.0 jit_solution(12314878707856874715)
XLA Ops:
  7.2 0.0 all-gather.3.cloned.1.call-start
  7.2 1.0 convert_element_type.7
  8.2 3.0 collective-permute-start
  11.2 1.0 collective-permute-start.1
  12.2 0.8 copy.38
  12.9 0.1 reshape.94
  13.0 0.1 broadcast.33.clone
  13.1 0.9 convert_dynamic-update-slice_fusion
  14.1 3.7 collective-permute-done
  17.9 1.1 collective-permute-start.2
  19.0 3.7 collective-permute-done.1
  22.7 2.8 collective-permute-done.2
  25.5 0.1 copy_bitcast_fusion.5
  25.5 0.7 gather_fusion
  26.2 1.1 bitcast_reduce_fusion.1
  27.3 1.0 copy_bitcast_fusion.3
  28.3 0.0 all-gather.3.cloned.1.call-update
  28.3 0.0 reduce-scatter.5.cloned.1.call-start
  28.4 65.4 %all-gather.3.cloned.1.call-done = f32[1536,1024]{1,0:T(8,128)} async-done(((f32[192,1024]{1,0:T(8,128)}), f32[1536,1024]{1,0:T(8,128)}) %all-gather.3.cloned.1.call-update) | async-done | bytes 6291472 | tf_op jit(solution)/shard_map/all_gather | solution.py:65
  93.8 8.0 %convert_multiply_fusion.3 = f32[1536,1024]{1,0:T(8,128)} fusion(f32[1536,1024]{1,0:T(8,128)} %all-gather.3.cloned.1.call-done, bf16[1,1536,1024]{2,1,0:T(8,128)(2,1)} %param.11), kind=kLoop, calls=%fused_computation.5 | loop fusion | flops 3145728 | bytes 15728640 | tf_op jit(solution)/shard_map/mul | solution.py:66
  101.8 3.2 reduce_sum.59
  105.1 3.2 fusion.19
  108.3 4.2 fusion.2
  112.6 3.5 convert_multiply_fusion.2
  116.1 0.2 reduce-scatter.7.cloned.1.call-start
  116.3 0.1 eq.41
  116.4 68.3 %reduce-scatter.5.cloned.1.call-done = f32[192,1024]{1,0:T(8,128)} async-done(((f32[1536,1024]{1,0:T(8,128)}), f32[192,1024]{1,0:T(8,128)}) %reduce-scatter.5.cloned.1.call-update) | async-done | bytes 786448 | tf_op jit(solution)/shard_map/reduce_scatter | solution.py:69
  184.7 1.3 copy.58
  186.0 0.8 fusion.26
  186.8 1.5 fusion.16
  188.3 1.0 copy.77
  189.4 0.0 reduce-scatter.7.cloned.1.call-update
  189.4 0.0 all-gather.5.cloned.1.call-start
  189.4 24.5 %reduce-scatter.7.cloned.1.call-done = f32[192,256]{1,0:T(8,128)} async-done(((f32[192,1024]{1,0:T(8,128)}), f32[192,256]{1,0:T(8,128)}) %reduce-scatter.7.cloned.1.call-update) | async-done | bytes 196624 | tf_op jit(solution)/shard_map/reduce_scatter | solution.py:86
  214.0 0.1 broadcast.33
  214.1 1.7 constant_dynamic-update-slice_fusion.3
  215.7 1.4 collective-permute-start.3
  217.2 1.5 collective-permute-start.4
  218.7 5.8 %collective-permute-done.3 = f32[192,256]{1,0:T(8,128)S(1)} collective-permute-done((f32[192,256]{1,0:T(8,128)S(1)}, f32[192,256]{1,0:T(8,128)S(1)}, u32[]{:S(2)}, u32[]{:S(2)}) %collective-permute-start.3) | collective-permute-done | bytes 196640 | tf_op jit(solution)/shard_map/ppermute | solution.py:42
  224.4 0.5 collective-permute-start.5
  225.0 3.6 collective-permute-done.4
  228.6 3.0 collective-permute-done.5
  231.7 0.1 copy_bitcast_fusion.4
  231.8 0.7 gather_fusion.1
  232.4 1.1 bitcast_reduce_fusion
  233.5 1.0 copy_bitcast_fusion.2
  234.5 0.0 all-gather.5.cloned.1.call-update
  234.5 0.0 reduce-scatter.9.cloned.1.call-start
  234.6 64.8 %all-gather.5.cloned.1.call-done = f32[1536,1024]{1,0:T(8,128)} async-done(((f32[192,1024]{1,0:T(8,128)}), f32[1536,1024]{1,0:T(8,128)}) %all-gather.5.cloned.1.call-update) | async-done | bytes 6291472 | tf_op jit(solution)/shard_map/all_gather | solution.py:65
  299.4 8.0 %convert_multiply_fusion.1 = f32[1536,1024]{1,0:T(8,128)} fusion(f32[1536,1024]{1,0:T(8,128)} %all-gather.5.cloned.1.call-done, bf16[1,1536,1024]{2,1,0:T(8,128)(2,1)} %param.11), kind=kLoop, calls=%fused_computation.3 | loop fusion | flops 3145728 | bytes 15728640 | tf_op jit(solution)/shard_map/mul | solution.py:66
  307.4 3.2 reduce_sum.63
  310.6 3.2 fusion.18
  313.8 4.2 fusion
  318.1 3.5 convert_multiply_fusion
  321.6 0.0 reduce-scatter.9.cloned.1.call-update
  321.6 0.0 reduce-scatter.11.cloned.1.call-start
  321.7 68.6 %reduce-scatter.9.cloned.1.call-done = f32[192,1024]{1,0:T(8,128)} async-done(((f32[1536,1024]{1,0:T(8,128)}), f32[192,1024]{1,0:T(8,128)}) %reduce-scatter.9.cloned.1.call-update) | async-done | bytes 786448 | tf_op jit(solution)/shard_map/reduce_scatter | solution.py:69
  390.2 1.3 copy.60
  391.5 0.8 fusion.24
  392.3 1.5 fusion.14
  393.8 1.0 copy.76
  394.8 0.0 reduce-scatter.11.cloned.1.call-update
  394.9 24.6 %reduce-scatter.11.cloned.1.call-done = f32[192,256]{1,0:T(8,128)} async-done(((f32[192,1024]{1,0:T(8,128)}), f32[192,256]{1,0:T(8,128)}) %reduce-scatter.11.cloned.1.call-update) | async-done | bytes 196624 | tf_op jit(solution)/shard_map/reduce_scatter | solution.py:86
  419.5 1.6 add.70
  (28 shorter events, 0.2 us)
Async XLA Ops:
  7.2 19.0 %copy-start = (bf16[8,2,128,128]{3,2,1,0:T(8,128)(2,1)S(1)}, bf16[8,2,128,128]{3,2,1,0:T(8,128)(2,1)}, u32[]{:S(2)}) copy-start(bf16[8,2,128,128]{3,2,1,0:T(8,128)(2,1)} %param.10) | copy-start | bytes 1572868
  7.2 86.6 %all-gather.3.cloned.1.call-start = ((), (), s32[]{:S(2)}) async-start(), calls=%async_computation.4 | async-start | bytes 7077888 | tf_op jit(solution)/shard_map/all_gather | solution.py:65
  8.2 9.7 %collective-permute-start = (f32[192,256]{1,0:T(8,128)S(1)}, f32[192,256]{1,0:T(8,128)S(1)}, u32[]{:S(2)}, u32[]{:S(2)}) collective-permute-start(f32[192,256]{1,0:T(8,128)S(1)} %convert_element_type.7), channel_id=1, source_target_pairs={{0,8},{8,16},{16,24},{24,0},{1,9},{9,17},{17,25},{25,1},{2,10},{10... | collective-permute-start | bytes 589832 | tf_op jit(solution)/shard_map/ppermute | solution.py:42
  11.2 11.5 %collective-permute-start.1 = (f32[192,256]{1,0:T(8,128)S(1)}, f32[192,256]{1,0:T(8,128)S(1)}, u32[]{:S(2)}, u32[]{:S(2)}) collective-permute-start(f32[192,256]{1,0:T(8,128)S(1)} %convert_element_type.7), channel_id=1, source_target_pairs={{0,24},{8,0},{16,8},{24,16},{1,25},{9,1},{17,9},{25,17},{2,26},{10... | collective-permute-start | bytes 589832 | tf_op jit(solution)/shard_map/ppermute | solution.py:47
  17.9 7.6 %collective-permute-start.2 = (f32[192,256]{1,0:T(8,128)S(1)}, f32[192,256]{1,0:T(8,128)S(1)}, u32[]{:S(2)}, u32[]{:S(2)}) collective-permute-start(f32[192,256]{1,0:T(8,128)S(1)} %collective-permute-done), channel_id=1, source_target_pairs={{0,8},{8,16},{16,24},{24,0},{1,9},{9,17},{17,25},{25,1},{2,10},{10... | collective-permute-start | bytes 589832 | tf_op jit(solution)/shard_map/ppermute | solution.py:42
  26.2 2.2 copy-start.6
  28.3 156.4 %reduce-scatter.5.cloned.1.call-start = ((), (), s32[]{:S(2)}) async-start(), calls=%async_computation.5 | async-start | bytes 7077888 | tf_op jit(solution)/shard_map/reduce_scatter | solution.py:69
  101.8 3.3 copy-start.7
  105.0 3.3 copy-start.4
  105.1 3.2 copy-start.5
  105.1 7.5 %copy-start.1 = (bf16[1,1536,1024]{2,1,0:T(8,128)(2,1)S(1)}, bf16[1,1536,1024]{2,1,0:T(8,128)(2,1)}, u32[]{:S(2)}) copy-start(bf16[1,1536,1024]{2,1,0:T(8,128)(2,1)} %param.11) | copy-start | bytes 9437188
  116.1 97.9 %reduce-scatter.7.cloned.1.call-start = ((), (), s32[]{:S(2)}) async-start(), calls=%async_computation.6 | async-start | bytes 983040 | tf_op jit(solution)/shard_map/reduce_scatter | solution.py:86
  188.3 25.8 %copy-start.3 = (bf16[192,256]{1,0:T(8,128)(2,1)S(1)}, bf16[192,256]{1,0:T(8,128)(2,1)}, u32[]{:S(2)}) copy-start(bf16[192,256]{1,0:T(8,128)(2,1)} %param.8) | copy-start | bytes 294916
  189.4 110.0 %all-gather.5.cloned.1.call-start = ((), (), s32[]{:S(2)}) async-start(), calls=%async_computation.7 | async-start | bytes 7077888 | tf_op jit(solution)/shard_map/all_gather | solution.py:65
  215.7 8.7 %collective-permute-start.3 = (f32[192,256]{1,0:T(8,128)S(1)}, f32[192,256]{1,0:T(8,128)S(1)}, u32[]{:S(2)}, u32[]{:S(2)}) collective-permute-start(f32[192,256]{1,0:T(8,128)S(1)} %get-tuple-element.3), channel_id=1, source_target_pairs={{0,8},{8,16},{16,24},{24,0},{1,9},{9,17},{17,25},{25,1},{2,10},{10... | collective-permute-start | bytes 589832 | tf_op jit(solution)/shard_map/ppermute | solution.py:42
  217.2 11.4 %collective-permute-start.4 = (f32[192,256]{1,0:T(8,128)S(1)}, f32[192,256]{1,0:T(8,128)S(1)}, u32[]{:S(2)}, u32[]{:S(2)}) collective-permute-start(f32[192,256]{1,0:T(8,128)S(1)} %get-tuple-element.3), channel_id=1, source_target_pairs={{0,24},{8,0},{16,8},{24,16},{1,25},{9,1},{17,9},{25,17},{2,26},{10... | collective-permute-start | bytes 589832 | tf_op jit(solution)/shard_map/ppermute | solution.py:47
  224.4 7.3 %collective-permute-start.5 = (f32[192,256]{1,0:T(8,128)S(1)}, f32[192,256]{1,0:T(8,128)S(1)}, u32[]{:S(2)}, u32[]{:S(2)}) collective-permute-start(f32[192,256]{1,0:T(8,128)S(1)} %collective-permute-done.3), channel_id=1, source_target_pairs={{0,8},{8,16},{16,24},{24,0},{1,9},{9,17},{17,25},{25,1},{2,10},{10... | collective-permute-start | bytes 589832 | tf_op jit(solution)/shard_map/ppermute | solution.py:42
  234.5 155.7 %reduce-scatter.9.cloned.1.call-start = ((), (), s32[]{:S(2)}) async-start(), calls=%async_computation.8 | async-start | bytes 7077888 | tf_op jit(solution)/shard_map/reduce_scatter | solution.py:69
  310.6 7.4 %copy-start.2 = (bf16[1,1536,1024]{2,1,0:T(8,128)(2,1)S(1)}, bf16[1,1536,1024]{2,1,0:T(8,128)(2,1)}, u32[]{:S(2)}) copy-start(bf16[1,1536,1024]{2,1,0:T(8,128)(2,1)} %param.11) | copy-start | bytes 9437188
  321.6 97.9 %reduce-scatter.11.cloned.1.call-start = ((), (), s32[]{:S(2)}) async-start(), calls=%async_computation.9 | async-start | bytes 983040 | tf_op jit(solution)/shard_map/reduce_scatter | solution.py:86
Sparse Core Ops, SparseCore 0:
  28.5 65.2 all-gather.2
  116.2 68.4 reduce-scatter.4
  189.5 24.4 reduce-scatter.6
  234.7 64.7 all-gather.4
  321.7 68.4 reduce-scatter.8
  395.0 24.4 reduce-scatter.10
